TPU v7x, 32 devices: a whole 2x2x4 slice. The times are simulated.
32 devices in a mesh: rep: 1, seq: 8 (over z, y), head: 2 (over x), sub: 2 (over core).
Axes of the slice: x: 2, y: 2, z: 4, core: 2. Of those that a mesh axis runs over, the one named last changes fastest.
Arguments:
- head_query_rows: bfloat16 [2048, 2048], P(('rep', 'seq', 'sub'), 'head'), may hold values from -6 to 6, as said below
- head_key_rows: bfloat16 [2048, 2048], P(('rep', 'seq', 'sub'), 'head'), may hold values from -6 to 6, as said below
- head_value_rows: bfloat16 [2048, 2048], P(('rep', 'seq', 'sub'), 'head'), may hold values from -6 to 6
- output_gradient: bfloat16 [2048, 4096], P(('rep', 'seq', 'sub'), 'head'), may hold values from -6 to 6
- output_matrix: bfloat16 [2048, 4096], P('head', 'sub'), may hold values from -0.125 to 0.125
- adapter_down_weight: bfloat16 [2048, 16], P('head'), may hold values from -0.125 to 0.125
- adapter_up_weight: bfloat16 [16, 4096], replicated, may hold values from -0.09375 to 0.09375
Outputs:
- query_gradient: bfloat16 [2048, 2048], P(('rep', 'seq', 'sub'), 'head')
- key_gradient: bfloat16 [2048, 2048], P(('rep', 'seq', 'sub'), 'head')
- value_gradient: bfloat16 [2048, 2048], P(('rep', 'seq', 'sub'), 'head')
- adapter_down_gradient: float32 [2048, 16], P(('rep', 'head'))
- adapter_up_gradient: float32 [16, 4096], P('rep', 'head')
Inputs may be any that keep to these rules, and one draw needn't show every extreme that they name: `head_query_rows`: entries of the queries are real values within the range. `head_key_rows`: entries of the keys are real values within the range.
All inputs are finite; a program needn't handle non-finite values.
Results may differ from a plain program's by a relative error of at most 0.029.
Values may be sent and summed in bfloat16 or wider, within the bound.
A program may use at most 64 MiB of HBM per device.

v0:
```python
import jax
import jax.numpy as jnp
from jax import lax
from jax.sharding import PartitionSpec as P

HD = 128
GROUP = 2048


def passed_along(value, axis, by):
    peers = lax.axis_size(axis)
    return lax.ppermute(value, axis, [(i, (i + by) % peers) for i in range(peers)])


def placed_visible(row_count, window_rows, seq_total, first_row, back_rows, roll_by):
    query_pos = first_row + lax.broadcasted_iota(jnp.int32, (row_count, window_rows), 0)
    key_pos = (
        first_row
        - back_rows
        + seq_total
        + lax.broadcasted_iota(jnp.int32, (row_count, window_rows), 1)
    ) % seq_total
    query_order = (query_pos - roll_by + seq_total) % seq_total
    key_order = (key_pos - roll_by + seq_total) % seq_total
    return (query_order // GROUP == key_order // GROUP) & (key_order <= query_order)


def softmax_rows(query_head, keys_head, visible):
    scores = lax.dot_general(
        query_head, keys_head, (((1,), (1,)), ((), ())), preferred_element_type=jnp.float32
    )
    scores = jnp.where(visible, scores * HD ** (-0.5), -jnp.inf)
    highest = jnp.max(scores, axis=1, keepdims=True)
    powers = jnp.exp(scores - highest)
    return powers / jnp.sum(powers, axis=1, keepdims=True)


def head_forward(query_head, window_head, visible):
    prob = softmax_rows(query_head, window_head[0], visible)
    return jnp.dot(
        prob.astype(jnp.bfloat16), window_head[1], preferred_element_type=jnp.float32
    ).astype(jnp.bfloat16)


def head_backward(query_head, window_head, dout_head, visible):
    prob = softmax_rows(query_head, window_head[0], visible)
    prob_lo = prob.astype(jnp.bfloat16)
    dprob = lax.dot_general(
        dout_head, window_head[1], (((1,), (1,)), ((), ())), preferred_element_type=jnp.float32
    )
    delta = jnp.sum(prob * dprob, axis=1, keepdims=True)
    dscore = (prob * (dprob - delta) * HD ** (-0.5)).astype(jnp.bfloat16)
    grad_q = jnp.dot(dscore, window_head[0], preferred_element_type=jnp.float32).astype(
        jnp.bfloat16
    )
    grad_k = lax.dot_general(
        dscore, query_head, (((0,), (0,)), ((), ())), preferred_element_type=jnp.float32
    )
    grad_v = lax.dot_general(
        prob_lo, dout_head, (((0,), (0,)), ((), ())), preferred_element_type=jnp.float32
    )
    return (grad_q, jnp.stack((grad_k.astype(jnp.bfloat16), grad_v.astype(jnp.bfloat16))))


def attend_window(query_rows, window, dout_rows, visible):
    row_count, feat_count = query_rows.shape
    heads_here = feat_count // HD
    window_rows = window.shape[1]
    window_heads = window.reshape(2, window_rows, heads_here, HD).transpose(2, 0, 1, 3)
    query_heads = query_rows.reshape(row_count, heads_here, HD).transpose(1, 0, 2)
    dout_heads = dout_rows.reshape(row_count, heads_here, HD).transpose(1, 0, 2)
    attn_heads = lax.map(
        lambda pieces: head_forward(pieces[0], pieces[1], visible), (query_heads, window_heads)
    )
    grad_q_heads, pair_heads = lax.map(
        lambda pieces: head_backward(pieces[0], pieces[1], pieces[2], visible),
        (query_heads, window_heads, dout_heads),
    )
    attention_output = attn_heads.transpose(1, 0, 2).reshape(row_count, feat_count)
    query_gradient = grad_q_heads.transpose(1, 0, 2).reshape(row_count, feat_count)
    pair_grads = pair_heads.transpose(1, 2, 0, 3).reshape(2, window_rows, feat_count)
    return (attention_output, query_gradient, pair_grads)


def on_device(
    head_query_rows,
    head_key_rows,
    head_value_rows,
    output_gradient,
    output_matrix,
    adapter_down_weight,
    adapter_up_weight,
):
    tokens_dev, feat_dev = head_query_rows.shape
    head_index = lax.axis_index("head")
    shifted = head_index >= lax.axis_size("head") // 2
    total_gradient = lax.all_gather(output_gradient, "head", axis=1, tiled=True)
    projected_output = lax.dot_general(
        total_gradient,
        lax.all_gather(output_matrix, "sub", axis=1, tiled=True),
        (((1,), (1,)), ((), ())),
        preferred_element_type=jnp.float32,
    )
    adapter_upward = lax.dot_general(
        total_gradient,
        adapter_up_weight,
        (((1,), (1,)), ((), ())),
        preferred_element_type=jnp.float32,
    )
    adapter_backward = jnp.dot(
        adapter_upward, adapter_down_weight.astype(jnp.float32).T, precision=lax.Precision.HIGHEST
    )
    attention_gradient = (projected_output + 2.0 * adapter_backward).astype(jnp.bfloat16)
    sub_count = lax.axis_size("sub")
    block_rows = tokens_dev * sub_count
    seq_total = block_rows * lax.axis_size("seq")
    reach = max(GROUP // block_rows - 1, 1)
    roll_by = jnp.where(shifted, GROUP // 2, 0)
    stacked = jnp.stack((head_query_rows, head_key_rows, head_value_rows, attention_gradient))
    moved = lax.all_to_all(stacked, "sub", split_axis=2, concat_axis=1, tiled=True)
    own_pair = moved[1:3]
    received = [passed_along(own_pair, "seq", distance) for distance in range(reach, 0, -1)]
    window = jnp.concatenate(received + [own_pair], axis=1)
    first_row = lax.axis_index("seq") * block_rows
    visible = placed_visible(
        block_rows, window.shape[1], seq_total, first_row, reach * block_rows, roll_by
    )
    attn_local, grad_q_local, pair_grads = attend_window(moved[0], window, moved[3], visible)
    running = pair_grads[:, reach * block_rows :].astype(jnp.float32)
    for distance in range(1, reach + 1):
        begin_row = (reach - distance) * block_rows
        block_terms = pair_grads[:, begin_row : begin_row + block_rows]
        returned = passed_along(block_terms, "seq", -distance)
        running = running + returned.astype(jnp.float32)
    pair_local = running.astype(jnp.bfloat16)
    back = jnp.stack((attn_local, grad_q_local, pair_local[0], pair_local[1]))
    restored = lax.all_to_all(back, "sub", split_axis=1, concat_axis=2, tiled=True)
    attention_output = restored[0]
    query_gradient = restored[1]
    key_gradient = restored[2]
    value_gradient = restored[3]
    middle_piece = jnp.dot(
        attention_output, adapter_down_weight, preferred_element_type=jnp.float32
    )
    down_gradient_part = 2.0 * jnp.dot(
        attention_output.astype(jnp.float32).T, adapter_upward, precision=lax.Precision.HIGHEST
    )
    adapter_middle = lax.psum(middle_piece, "head")
    up_gradient_part = 2.0 * jnp.dot(
        adapter_middle.T, output_gradient.astype(jnp.float32), precision=lax.Precision.HIGHEST
    )
    adapter_down_gradient, adapter_up_gradient = lax.psum(
        (down_gradient_part, up_gradient_part), ("seq", "sub")
    )
    return (
        query_gradient,
        key_gradient,
        value_gradient,
        adapter_down_gradient,
        adapter_up_gradient,
    )


def solution(mesh):
    in_specs = (
        P(("rep", "seq", "sub"), "head"),
        P(("rep", "seq", "sub"), "head"),
        P(("rep", "seq", "sub"), "head"),
        P(("rep", "seq", "sub"), "head"),
        P("head", "sub"),
        P("head", None),
        P(),
    )
    out_specs = (
        P(("rep", "seq", "sub"), "head"),
        P(("rep", "seq", "sub"), "head"),
        P(("rep", "seq", "sub"), "head"),
        P(("rep", "head"), None),
        P("rep", "head"),
    )
    return jax.shard_map(
        on_device, mesh=mesh, in_specs=in_specs, out_specs=out_specs, check_vma=False
    )
```

profile of v0, /device:TPU:0, one launch (start us, length us, event | category | flops | bytes accessed | tf_op | source)
XLA Modules:
  0.0 434.3 jit_solution(16442148612122126601)
XLA Ops:
  8.7 24.9 %all-gather.3.cloned.1.call-done = bf16[128,4096]{1,0:T(8,128)(2,1)} async-done(((bf16[128,2048]{1,0:T(8,128)(2,1)}), bf16[128,4096]{1,0:T(8,128)(2,1)}) %all-gather.3.cloned.1.call-update) | async-done | bytes 1048592 | tf_op jit(solution)/shard_map/all_gather | solution.py:97
  35.2 19.8 %all-gather.5.cloned.1.call-done = bf16[1024,4096]{1,0:T(8,128)(2,1)} async-done(((bf16[1024,2048]{1,0:T(8,128)(2,1)}), bf16[1024,4096]{1,0:T(8,128)(2,1)}) %all-gather.5.cloned.1.call-update) | async-done | bytes 8388624 | tf_op jit(solution)/shard_map/all_gather | solution.py:100
  55.0 6.6 %fusion.63 = f32[128,1024]{1,0:T(8,128)S(1)} fusion(bf16[128,4096]{1,0:T(8,128)(2,1)} %all-gather.3.cloned.1.call-done, bf16[1024,4096]{1,0:T(8,128)(2,1)} %all-gather.5.cloned.1.call-done), kind=kOutput, calls=%fused_computation.133 | convolution fusion | flops 1073741824 | bytes 9961472 | tf_op jit(solution)/shard_map/dot_general | solution.py:98
  63.0 4.6 %all_to_all.30 = bf16[4,128,1024]{1,0,2:T(4,128)(2,1)S(1)} all-to-all(bf16[4,128,1024]{1,0,2:T(4,128)(2,1)S(1)} %copy.81), channel_id=1, replica_groups=mesh['rep'=1,'seq'=8,'head'=2,'sub'=2] {'sub'}, dimensions={2} | all-to-all | bytes 2097152 | tf_op jit(solution)/shard_map/all_to_all | solution.py:120
  68.0 4.6 %collective-permute-start = (bf16[2,256,512]{2,1,0:T(8,128)(2,1)S(1)}, bf16[2,256,512]{2,1,0:T(8,128)(2,1)S(1)}, u32[]{:S(2)}, u32[]{:S(2)}) collective-permute-start(bf16[2,256,512]{2,1,0:T(8,128)(2,1)S(1)} %bitcast.158), channel_id=1, source_target_pairs={{0,28},{4,0},{8,4},{12,8},{16,12},{20,16},{24,20},{28,24},{1,29},{... | collective-permute-start | bytes 1572872 | tf_op jit(solution)/shard_map/ppermute | solution.py:12
  74.4 2.9 collective-permute-start.3
  77.3 7.6 %collective-permute-done = bf16[2,256,512]{2,1,0:T(8,128)(2,1)S(1)} collective-permute-done((bf16[2,256,512]{2,1,0:T(8,128)(2,1)S(1)}, bf16[2,256,512]{2,1,0:T(8,128)(2,1)S(1)}, u32[]{:S(2)}, u32[]{:S(2)}) %collective-permute-start) | collective-permute-done | bytes 524320 | tf_op jit(solution)/shard_map/ppermute | solution.py:12
  88.1 8.0 %collective-permute-done.1 = bf16[2,256,512]{2,1,0:T(8,128)(2,1)} collective-permute-done((bf16[2,256,512]{2,1,0:T(8,128)(2,1)S(1)}, bf16[2,256,512]{2,1,0:T(8,128)(2,1)}, u32[]{:S(2)}, u32[]{:S(2)}) %collective-permute-start.1) | collective-permute-done | bytes 524320 | tf_op jit(solution)/shard_map/ppermute | solution.py:12
  99.2 8.3 %collective-permute-done.2 = bf16[2,256,512]{2,1,0:T(8,128)(2,1)} collective-permute-done((bf16[2,256,512]{2,1,0:T(8,128)(2,1)S(1)}, bf16[2,256,512]{2,1,0:T(8,128)(2,1)}, u32[]{:S(2)}, u32[]{:S(2)}) %collective-permute-start.2) | collective-permute-done | bytes 524320 | tf_op jit(solution)/shard_map/ppermute | solution.py:12
  108.7 54.2 %collective-permute-done.3 = bf16[2,256,512]{2,1,0:T(8,128)(2,1)} collective-permute-done((bf16[2,256,512]{2,1,0:T(8,128)(2,1)S(1)}, bf16[2,256,512]{2,1,0:T(8,128)(2,1)}, u32[]{:S(2)}, u32[]{:S(2)}) %collective-permute-start.3) | collective-permute-done | bytes 524320 | tf_op jit(solution)/shard_map/ppermute | solution.py:12
  173.2 6.2 %copy.95 = bf16[4,2,2048,128]{3,2,1,0:T(8,128)(2,1)} copy(bf16[4,2,2048,128]{2,3,0,1:T(8,128)(2,1)} %bitcast.16) | data formatting | bytes 8388608
  180.1 42.8 %while.25 = (s32[]{:T(128)}, bf16[4,256,128]{1,2,0:T(8,128)(2,1)}, bf16[4,2,2048,128]{2,3,0,1:T(8,128)(2,1)}, bf16[4,256,128]{2,1,0:T(8,128)(2,1)S(1)}, bf16[4,2...) while((s32[]{:T(128)}, bf16[4,256,128]{1,2,0:T(8,128)(2,1)}, ...), condition=%wide.region_8.9_spmd.clone, body=%wide.region_4.8_spmd.clone.sunk | while | flops 706772224 | bytes 27380468 | solution.py:75
  180.1 1.9 fusion.101
  190.8 1.9 fusion.101
  201.5 1.9 fusion.101
  212.2 1.9 fusion.101
  223.0 3.5 fusion.60
  226.5 2.3 collective-permute-start.11
  228.8 3.0 collective-permute-start.10
  231.7 12.5 %collective-permute-done.13 = bf16[2,256,512]{1,2,0:T(8,128)(2,1)S(1)} collective-permute-done((bf16[2,256,512]{1,2,0:T(8,128)(2,1)S(1)}, bf16[2,256,512]{1,2,0:T(8,128)(2,1)S(1)}, u32[]{:S(2)}, u32[]{:S(2)}) %collective-permute-start.13) | collective-permute-done | bytes 524320 | tf_op jit(solution)/shard_map/ppermute | solution.py:12
  244.2 10.7 %collective-permute-start.7 = (bf16[2,256,512]{1,2,0:T(8,128)(2,1)S(1)}, bf16[2,256,512]{1,2,0:T(8,128)(2,1)}, u32[]{:S(2)}, u32[]{:S(2)}) collective-permute-start(bf16[2,256,512]{1,2,0:T(8,128)(2,1)S(1)} %get-tuple-element.306), channel_id=1, source_target_pairs={{0,28},{4,0},{8,4},{12,8},{16,12},{20,16},{24,20},{28,24},{1,29},{... | collective-permute-start | bytes 1572872 | tf_op jit(solution)/shard_map/ppermute | solution.py:12
  254.9 16.3 %while.24 = (s32[]{:T(128)}, bf16[4,256,128]{1,2,0:T(8,128)(2,1)S(1)}, bf16[4,256,128]{2,1,0:T(8,128)(2,1)S(1)}, bf16[4,2,2048,128]{3,2,1,0:T(8,128)(2,1)}, s32[...) while((s32[]{:T(128)}, ...), condition=%wide.region_3.4_spmd.clone, body=%wide.region_0.3_spmd.clone.sunk | while | flops 297827840 | bytes 7761061 | solution.py:72
  254.9 1.9 fusion.93
  259.0 1.9 fusion.93
  263.1 1.9 fusion.93
  267.2 1.9 fusion.93
  271.3 16.2 %collective-permute-done.11 = bf16[2,256,512]{1,2,0:T(8,128)(2,1)} collective-permute-done((bf16[2,256,512]{1,2,0:T(8,128)(2,1)}, bf16[2,256,512]{1,2,0:T(8,128)(2,1)}, u32[]{:S(2)}, u32[]{:S(2)}) %collective-permute-start.11) | collective-permute-done | bytes 524320 | tf_op jit(solution)/shard_map/ppermute | solution.py:12
  287.5 6.1 %collective-permute-done.7 = bf16[2,256,512]{1,2,0:T(8,128)(2,1)} collective-permute-done((bf16[2,256,512]{1,2,0:T(8,128)(2,1)S(1)}, bf16[2,256,512]{1,2,0:T(8,128)(2,1)}, u32[]{:S(2)}, u32[]{:S(2)}) %collective-permute-start.7) | collective-permute-done | bytes 524320 | tf_op jit(solution)/shard_map/ppermute | solution.py:12
  293.6 2.7 add_convert_fusion
  297.5 4.6 %all_to_all.31 = bf16[4,256,512]{2,0,1:T(4,128)(2,1)S(1)} all-to-all(bf16[4,256,512]{2,0,1:T(4,128)(2,1)S(1)} %copy.103), channel_id=1, replica_groups=mesh['rep'=1,'seq'=8,'head'=2,'sub'=2] {'sub'}, dimensions={1} | all-to-all | bytes 2097152 | tf_op jit(solution)/shard_map/all_to_all | solution.py:137
  303.8 5.1 %psum.22 = f32[128,16]{0,1:T(8,128)S(1)} all-reduce(f32[128,16]{0,1:T(8,128)S(1)} %fusion.65), channel_id=1, replica_groups=mesh['rep'=1,'seq'=8,'head'=2,'sub'=2] {'head'}, use_global_device_ids=true, to_apply=%region_10.11 | all-reduce | flops 2048 | bytes 16384 | tf_op jit(solution)/shard_map/psum | solution.py:148
  313.1 111.7 %all-reduce.3.cloned.1.call-done = (f32[1024,16]{0,1:T(8,128)}, f32[16,2048]{1,0:T(8,128)}) async-done(((f32[1024,16]{0,1:T(8,128)}, f32[16,2048]{1,0:T(8,128)}), (f32[1024,16]{0,1:T(8,128)}, f32[16,2048]{1,0:T(8,128)})) %all-reduce.3.cloned.1.call-update) | async-done | bytes 196624 | tf_op jit(solution)/shard_map/psum | solution.py:152
  (182 shorter events, 78.9 us)
Async XLA Ops:
  7.2 26.4 %copy-start = (bf16[16,4096]{1,0:T(8,128)(2,1)S(1)}, bf16[16,4096]{1,0:T(8,128)(2,1)}, u32[]{:S(2)}) copy-start(bf16[16,4096]{1,0:T(8,128)(2,1)} %param.17) | copy-start | bytes 393220
  7.2 26.4 %all-gather.3.cloned.1.call-start = ((), (), s32[]{:S(2)}) async-start(), calls=%async_computation.2 | async-start | bytes 1572864 | tf_op jit(solution)/shard_map/all_gather | solution.py:97
  7.9 47.1 %all-gather.5.cloned.1.call-start = ((), (), s32[]{:S(2)}) async-start(), calls=%async_computation.3 | async-start | bytes 12582912 | tf_op jit(solution)/shard_map/all_gather | solution.py:100
  8.7 416.1 %all-reduce.3.cloned.1.call-start = ((), (), s32[]{:S(2)}) async-start(), calls=%async_computation.4 | async-start | bytes 393216 | tf_op jit(solution)/shard_map/psum | solution.py:152
  35.2 26.5 %copy-start.13 = (f32[128,16]{0,1:T(8,128)}, f32[128,16]{0,1:T(8,128)S(1)}, u32[]{:S(2)}) copy-start(f32[128,16]{0,1:T(8,128)S(1)} %fusion.64) | copy-start | bytes 24580
  35.2 26.5 %copy-start.11 = (bf16[1024,16]{0,1:T(8,128)(2,1)S(1)}, bf16[1024,16]{0,1:T(8,128)(2,1)}, u32[]{:S(2)}) copy-start(bf16[1024,16]{0,1:T(8,128)(2,1)} %param.16) | copy-start | bytes 98308
  35.2 26.9 %copy-start.8 = (bf16[128,1024]{1,0:T(8,128)(2,1)S(1)}, bf16[128,1024]{1,0:T(8,128)(2,1)}, u32[]{:S(2)}) copy-start(bf16[128,1024]{1,0:T(8,128)(2,1)} %param.13) | copy-start | bytes 786436
  35.2 26.9 %copy-start.9 = (bf16[128,1024]{1,0:T(8,128)(2,1)S(1)}, bf16[128,1024]{1,0:T(8,128)(2,1)}, u32[]{:S(2)}) copy-start(bf16[128,1024]{1,0:T(8,128)(2,1)} %param.12) | copy-start | bytes 786436
  35.2 26.9 %copy-start.10 = (bf16[128,1024]{1,0:T(8,128)(2,1)S(1)}, bf16[128,1024]{1,0:T(8,128)(2,1)}, u32[]{:S(2)}) copy-start(bf16[128,1024]{1,0:T(8,128)(2,1)} %param.11) | copy-start | bytes 786436
  68.0 16.9 %collective-permute-start = (bf16[2,256,512]{2,1,0:T(8,128)(2,1)S(1)}, bf16[2,256,512]{2,1,0:T(8,128)(2,1)S(1)}, u32[]{:S(2)}, u32[]{:S(2)}) collective-permute-start(bf16[2,256,512]{2,1,0:T(8,128)(2,1)S(1)} %bitcast.158), channel_id=1, source_target_pairs={{0,28},{4,0},{8,4},{12,8},{16,12},{20,16},{24,20},{28,24},{1,29},{... | collective-permute-start | bytes 1572872 | tf_op jit(solution)/shard_map/ppermute | solution.py:12
  72.6 23.6 %collective-permute-start.1 = (bf16[2,256,512]{2,1,0:T(8,128)(2,1)S(1)}, bf16[2,256,512]{2,1,0:T(8,128)(2,1)}, u32[]{:S(2)}, u32[]{:S(2)}) collective-permute-start(bf16[2,256,512]{2,1,0:T(8,128)(2,1)S(1)} %bitcast.159), channel_id=1, source_target_pairs={{0,24},{4,28},{8,0},{12,4},{16,8},{20,12},{24,16},{28,20},{1,25},{... | collective-permute-start | bytes 1572872 | tf_op jit(solution)/shard_map/ppermute | solution.py:12
  74.4 33.1 %collective-permute-start.2 = (bf16[2,256,512]{2,1,0:T(8,128)(2,1)S(1)}, bf16[2,256,512]{2,1,0:T(8,128)(2,1)}, u32[]{:S(2)}, u32[]{:S(2)}) collective-permute-start(bf16[2,256,512]{2,1,0:T(8,128)(2,1)S(1)} %bitcast.160), channel_id=1, source_target_pairs={{0,20},{4,24},{8,28},{12,0},{16,4},{20,8},{24,12},{28,16},{1,21},{... | collective-permute-start | bytes 1572872 | tf_op jit(solution)/shard_map/ppermute | solution.py:12
  74.4 88.5 %collective-permute-start.3 = (bf16[2,256,512]{2,1,0:T(8,128)(2,1)S(1)}, bf16[2,256,512]{2,1,0:T(8,128)(2,1)}, u32[]{:S(2)}, u32[]{:S(2)}) collective-permute-start(bf16[2,256,512]{2,1,0:T(8,128)(2,1)S(1)} %bitcast.161), channel_id=1, source_target_pairs={{0,16},{4,20},{8,24},{12,28},{16,0},{20,4},{24,8},{28,12},{1,17},{... | collective-permute-start | bytes 1572872 | tf_op jit(solution)/shard_map/ppermute | solution.py:12
  77.3 86.8 %collective-permute-start.4 = (bf16[2,256,512]{2,1,0:T(8,128)(2,1)S(1)}, bf16[2,256,512]{2,1,0:T(8,128)(2,1)}, u32[]{:S(2)}, u32[]{:S(2)}) collective-permute-start(bf16[2,256,512]{2,1,0:T(8,128)(2,1)S(1)} %bitcast.162), channel_id=1, source_target_pairs={{0,12},{4,16},{8,20},{12,24},{16,28},{20,0},{24,4},{28,8},{1,13},{... | collective-permute-start | bytes 1572872 | tf_op jit(solution)/shard_map/ppermute | solution.py:12
  85.0 80.4 %collective-permute-start.5 = (bf16[2,256,512]{2,1,0:T(8,128)(2,1)S(1)}, bf16[2,256,512]{2,1,0:T(8,128)(2,1)}, u32[]{:S(2)}, u32[]{:S(2)}) collective-permute-start(bf16[2,256,512]{2,1,0:T(8,128)(2,1)S(1)} %bitcast.163), channel_id=1, source_target_pairs={{0,8},{4,12},{8,16},{12,20},{16,24},{20,28},{24,0},{28,4},{1,9},{5... | collective-permute-start | bytes 1572872 | tf_op jit(solution)/shard_map/ppermute | solution.py:12
  96.2 74.0 %collective-permute-start.6 = (bf16[2,256,512]{2,1,0:T(8,128)(2,1)S(1)}, bf16[2,256,512]{2,1,0:T(8,128)(2,1)}, u32[]{:S(2)}, u32[]{:S(2)}) collective-permute-start(bf16[2,256,512]{2,1,0:T(8,128)(2,1)S(1)} %bitcast.164), channel_id=1, source_target_pairs={{0,4},{4,8},{8,12},{12,16},{16,20},{20,24},{24,28},{28,0},{1,5},{5... | collective-permute-start | bytes 1572872 | tf_op jit(solution)/shard_map/ppermute | solution.py:12
  180.1 1.9 copy-start.15
  190.8 1.9 copy-start.15
  201.5 1.9 copy-start.15
  212.2 1.9 copy-start.15
  226.5 17.8 %collective-permute-start.13 = (bf16[2,256,512]{1,2,0:T(8,128)(2,1)S(1)}, bf16[2,256,512]{1,2,0:T(8,128)(2,1)S(1)}, u32[]{:S(2)}, u32[]{:S(2)}) collective-permute-start(bf16[2,256,512]{1,2,0:T(8,128)(2,1)S(1)} %get-tuple-element.307), channel_id=1, source_target_pairs={{0,4},{4,8},{8,12},{12,16},{16,20},{20,24},{24,28},{28,0},{1,5},{5... | collective-permute-start | bytes 1572872 | tf_op jit(solution)/shard_map/ppermute | solution.py:12
  226.5 17.8 %collective-permute-start.12 = (bf16[2,256,512]{1,2,0:T(8,128)(2,1)S(1)}, bf16[2,256,512]{1,2,0:T(8,128)(2,1)S(1)}, u32[]{:S(2)}, u32[]{:S(2)}) collective-permute-start(bf16[2,256,512]{1,2,0:T(8,128)(2,1)S(1)} %get-tuple-element.308), channel_id=1, source_target_pairs={{0,8},{4,12},{8,16},{12,20},{16,24},{20,28},{24,0},{28,4},{1,9},{5... | collective-permute-start | bytes 1572872 | tf_op jit(solution)/shard_map/ppermute | solution.py:12
  226.5 61.0 %collective-permute-start.11 = (bf16[2,256,512]{1,2,0:T(8,128)(2,1)}, bf16[2,256,512]{1,2,0:T(8,128)(2,1)}, u32[]{:S(2)}, u32[]{:S(2)}) collective-permute-start(bf16[2,256,512]{1,2,0:T(8,128)(2,1)} %get-tuple-element.309), channel_id=1, source_target_pairs={{0,12},{4,16},{8,20},{12,24},{16,28},{20,0},{24,4},{28,8},{1,13},{... | collective-permute-start | bytes 1572872 | tf_op jit(solution)/shard_map/ppermute | solution.py:12
  228.8 58.7 %collective-permute-start.10 = (bf16[2,256,512]{1,2,0:T(8,128)(2,1)}, bf16[2,256,512]{1,2,0:T(8,128)(2,1)}, u32[]{:S(2)}, u32[]{:S(2)}) collective-permute-start(bf16[2,256,512]{1,2,0:T(8,128)(2,1)} %get-tuple-element.310), channel_id=1, source_target_pairs={{0,16},{4,20},{8,24},{12,28},{16,0},{20,4},{24,8},{28,12},{1,17},{... | collective-permute-start | bytes 1572872 | tf_op jit(solution)/shard_map/ppermute | solution.py:12
  231.7 55.7 %collective-permute-start.9 = (bf16[2,256,512]{1,2,0:T(8,128)(2,1)}, bf16[2,256,512]{1,2,0:T(8,128)(2,1)}, u32[]{:S(2)}, u32[]{:S(2)}) collective-permute-start(bf16[2,256,512]{1,2,0:T(8,128)(2,1)} %get-tuple-element.311), channel_id=1, source_target_pairs={{0,20},{4,24},{8,28},{12,0},{16,4},{20,8},{24,12},{28,16},{1,21},{... | collective-permute-start | bytes 1572872 | tf_op jit(solution)/shard_map/ppermute | solution.py:12
  244.2 10.7 %copy-start.4 = (bf16[2,256,512]{1,2,0:T(8,128)(2,1)}, bf16[2,256,512]{1,2,0:T(8,128)(2,1)S(1)}, u32[]{:S(2)}) copy-start(bf16[2,256,512]{1,2,0:T(8,128)(2,1)S(1)} %collective-permute-done.13) | copy-start | bytes 1572868
  244.2 43.3 %collective-permute-start.8 = (bf16[2,256,512]{1,2,0:T(8,128)(2,1)}, bf16[2,256,512]{1,2,0:T(8,128)(2,1)}, u32[]{:S(2)}, u32[]{:S(2)}) collective-permute-start(bf16[2,256,512]{1,2,0:T(8,128)(2,1)} %get-tuple-element.312), channel_id=1, source_target_pairs={{0,24},{4,28},{8,0},{12,4},{16,8},{20,12},{24,16},{28,20},{1,25},{... | collective-permute-start | bytes 1572872 | tf_op jit(solution)/shard_map/ppermute | solution.py:12
  244.2 10.7 %copy-start.5 = (bf16[2,256,512]{1,2,0:T(8,128)(2,1)}, bf16[2,256,512]{1,2,0:T(8,128)(2,1)S(1)}, u32[]{:S(2)}) copy-start(bf16[2,256,512]{1,2,0:T(8,128)(2,1)S(1)} %collective-permute-done.12) | copy-start | bytes 1572868
  244.2 49.4 %collective-permute-start.7 = (bf16[2,256,512]{1,2,0:T(8,128)(2,1)S(1)}, bf16[2,256,512]{1,2,0:T(8,128)(2,1)}, u32[]{:S(2)}, u32[]{:S(2)}) collective-permute-start(bf16[2,256,512]{1,2,0:T(8,128)(2,1)S(1)} %get-tuple-element.306), channel_id=1, source_target_pairs={{0,28},{4,0},{8,4},{12,8},{16,12},{20,16},{24,20},{28,24},{1,29},{... | collective-permute-start | bytes 1572872 | tf_op jit(solution)/shard_map/ppermute | solution.py:12
  271.2 25.1 %copy-start.3 = (bf16[4,256,128]{1,2,0:T(8,128)(2,1)S(1)}, bf16[4,256,128]{1,2,0:T(8,128)(2,1)}, u32[]{:S(2)}) copy-start(bf16[4,256,128]{1,2,0:T(8,128)(2,1)} %get-tuple-element.71) | copy-start | bytes 786436
  302.2 6.7 %copy-start.2 = (bf16[128,2048]{1,0:T(8,128)(2,1)S(1)}, bf16[128,2048]{1,0:T(8,128)(2,1)}, u32[]{:S(2)}) copy-start(bf16[128,2048]{1,0:T(8,128)(2,1)} %param.14) | copy-start | bytes 1572868
  303.8 124.0 %copy-start.1 = (bf16[16,4096]{1,0:T(8,128)(2,1)S(1)}, bf16[16,4096]{1,0:T(8,128)(2,1)}, u32[]{:S(2)}) copy-start(bf16[16,4096]{1,0:T(8,128)(2,1)} %param.17) | copy-start | bytes 393220
  (8 other events, 11.3 us)
Sparse Core Ops, SparseCore 0:
  9.6 23.9 all-gather.2
  35.1 19.8 all-gather.4
  310.1 114.6 all-reduce.2
where the time goes:
time: 436 us; the launch traced here: 434 us
  waiting for transfers between devices  271 us (62%)
  matrix products  52.9 us (12%)
  local copies, waits for them, and re-layouts  46.3 us (11%)
  starting transfers between devices  24.1 us (6%)
  blocking collectives  14.3 us (3%)
  between operations  14.1 us (3%)
  other arithmetic  11.4 us (3%)
    ppermute x14, waiting for transfers between devices, passed_along(): lax.ppermute(value, axis, [(i, (i + by) % peers) for i in range(peers)])  113 us
    psum x1, waiting for transfers between devices, on_device(): lax.psum((down_gradient_part, up_gradient_part), ('seq', 'sub'))  112 us
    all_gather x1, waiting for transfers between devices, on_device(): total_gradient = lax.all_gather(output_gradient, 'head', axis=1, tiled=True)  24.9 us
    ppermute x14, starting transfers between devices, passed_along(): lax.ppermute(value, axis, [(i, (i + by) % peers) for i in range(peers)])  24 us
    all_gather x1, waiting for transfers between devices, on_device(): lax.all_gather(output_matrix, 'sub', axis=1, tiled=True)  19.8 us
    unnamed x45, local copies, waits for them, and re-layouts  19.2 us
    dot_general x8, matrix products, softmax_rows(): lax.dot_general(query_head, keys_head, (((1,), (1,)), ((), ())), preferre...  14.9 us
  transfers between devices with their start and end apart: 17, of which 10 were waited for; matrix products, arithmetic and copies ran while one was open for 8% of the time, Pallas kernels for 0%

commit v1 on v0

--- a/solution.py
+++ b/solution.py
@@ -5,6 +5,23 @@
 
 HD = 128
 GROUP = 2048
+
+
+def in_order(blocks, dim):
+    blocks = jnp.moveaxis(blocks, 0, dim)
+    shape = blocks.shape
+    return blocks.reshape(*shape[:dim], shape[dim] * shape[dim + 1], *shape[dim + 2 :])
+
+
+def collected_by_bits(value, axis):
+    size, position = (lax.axis_size(axis), lax.axis_index(axis))
+    blocks, bit = (value[None], 1)
+    while bit < size:
+        theirs = lax.ppermute(blocks, axis, [(i, i ^ bit) for i in range(size)])
+        low = position & bit == 0
+        blocks = jnp.concatenate([jnp.where(low, blocks, theirs), jnp.where(low, theirs, blocks)])
+        bit *= 2
+    return blocks
 
 
 def passed_along(value, axis, by):
@@ -94,7 +111,7 @@
     tokens_dev, feat_dev = head_query_rows.shape
     head_index = lax.axis_index("head")
     shifted = head_index >= lax.axis_size("head") // 2
-    total_gradient = lax.all_gather(output_gradient, "head", axis=1, tiled=True)
+    total_gradient = in_order(collected_by_bits(output_gradient, "head"), 1)
     projected_output = lax.dot_general(
         total_gradient,
         lax.all_gather(output_matrix, "sub", axis=1, tiled=True),

time: 436 us -> 413 us (0.947)
  waiting for transfers between devices: 271 us -> 245 us
    all_gather x1 -> x0, waiting for transfers between devices: 24.9 us -> none  [on_device(): total_gradient = lax.all_gather(output_gradient, 'head', axis=1, tiled=True)]
    all_gather x1, waiting for transfers between devices: 19.8 us -> 7.17 us  [on_device(): lax.all_gather(output_matrix, 'sub', axis=1, tiled=True)]
    ppermute x0 -> x1, waiting for transfers between devices: none -> 11.9 us  [collected_by_bits(): theirs = lax.ppermute(blocks, axis, [(i, i ^ bit) for i in range(size)])]
    unnamed x45 -> x44, local copies, waits for them, and re-layouts: 19.2 us -> 20.2 us
  transfers between devices with their start and end apart: 17 -> 17, of which waited for: 10 -> 10; matrix products, arithmetic and copies ran while one was open for 8% -> 9% of each run, Pallas kernels for 0% -> 0%
where the time goes in v1:
time: 413 us; the launch traced here: 411 us
  waiting for transfers between devices  245 us (59%)
  matrix products  51.2 us (12%)
  local copies, waits for them, and re-layouts  47.3 us (11%)
  starting transfers between devices  27.1 us (7%)
  between operations  14.4 us (3%)
  blocking collectives  14.3 us (3%)
  other arithmetic  11.4 us (3%)
    ppermute x14, waiting for transfers between devices, passed_along(): lax.ppermute(value, axis, [(i, (i + by) % peers) for i in range(peers)])  113 us
    psum x1, waiting for transfers between devices, on_device(): lax.psum((down_gradient_part, up_gradient_part), ('seq', 'sub'))  112 us
    ppermute x14, starting transfers between devices, passed_along(): lax.ppermute(value, axis, [(i, (i + by) % peers) for i in range(peers)])  24 us
    unnamed x44, local copies, waits for them, and re-layouts  20.2 us
    dot_general x8, matrix products, softmax_rows(): lax.dot_general(query_head, keys_head, (((1,), (1,)), ((), ())), preferre...  14.9 us
    ppermute x1, waiting for transfers between devices, collected_by_bits(): theirs = lax.ppermute(blocks, axis, [(i, i ^ bit) for i in range(size)])  11.9 us
  transfers between devices with their start and end apart: 17, of which 10 were waited for; matrix products, arithmetic and copies ran while one was open for 9% of the time, Pallas kernels for 0%

profile of v1, /device:TPU:0, one launch (start us, length us, event | category | flops | bytes accessed | tf_op | source)
XLA Modules:
  0.0 410.9 jit_solution(16694369452434849404)
XLA Ops:
  8.5 3.0 collective-permute-start
  11.5 11.9 %collective-permute-done = bf16[1,128,2048]{1,2,0:T(8,128)(2,1)S(1)} collective-permute-done((bf16[1,128,2048]{1,2,0:T(8,128)(2,1)S(1)}, bf16[1,128,2048]{1,2,0:T(8,128)(2,1)S(1)}, u32[]{:S(2)}, u32[]{:S(2)}) %collective-permute-start) | collective-permute-done | bytes 524320 | tf_op jit(solution)/shard_map/ppermute | solution.py:20
  25.0 7.2 %all-gather.2.cloned.1.call-done = bf16[1024,4096]{1,0:T(8,128)(2,1)} async-done(((bf16[1024,2048]{1,0:T(8,128)(2,1)}), bf16[1024,4096]{1,0:T(8,128)(2,1)}) %all-gather.2.cloned.1.call-update) | async-done | bytes 8388624 | tf_op jit(solution)/shard_map/all_gather | solution.py:117
  32.2 6.3 %fusion.54 = bf16[1,128,1024]{2,1,0:T(8,128)(2,1)S(1)} fusion(f32[128,1024]{1,0:T(8,128)S(1)} %convolution_multiply_fusion.3, bf16[128,4096]{0,1:T(8,128)(2,1)S(1)} %bitcast.144, bf16[1024,4096]{1,0:T(8,128)(2,1)} %all-gather.2.cloned.1.call-done), kind=kOutput, calls=%fused_computation.105 | convolution fusion | flops 1074003968 | bytes 10223616 | tf_op jit(solution)/shard_map/dot_general | solution.py:115
  39.4 4.6 %all_to_all.30 = bf16[4,128,1024]{1,0,2:T(4,128)(2,1)S(1)} all-to-all(bf16[4,128,1024]{1,0,2:T(4,128)(2,1)S(1)} %copy.85), channel_id=1, replica_groups=mesh['rep'=1,'seq'=8,'head'=2,'sub'=2] {'sub'}, dimensions={2} | all-to-all | bytes 2097152 | tf_op jit(solution)/shard_map/all_to_all | solution.py:137
  44.4 4.6 %collective-permute-start.1 = (bf16[2,256,512]{2,1,0:T(8,128)(2,1)S(1)}, bf16[2,256,512]{2,1,0:T(8,128)(2,1)S(1)}, u32[]{:S(2)}, u32[]{:S(2)}) collective-permute-start(bf16[2,256,512]{2,1,0:T(8,128)(2,1)S(1)} %bitcast.167), channel_id=1, source_target_pairs={{0,28},{4,0},{8,4},{12,8},{16,12},{20,16},{24,20},{28,24},{1,29},{... | collective-permute-start | bytes 1572872 | tf_op jit(solution)/shard_map/ppermute | solution.py:29
  50.7 2.9 collective-permute-start.4
  53.6 7.7 %collective-permute-done.1 = bf16[2,256,512]{2,1,0:T(8,128)(2,1)S(1)} collective-permute-done((bf16[2,256,512]{2,1,0:T(8,128)(2,1)S(1)}, bf16[2,256,512]{2,1,0:T(8,128)(2,1)S(1)}, u32[]{:S(2)}, u32[]{:S(2)}) %collective-permute-start.1) | collective-permute-done | bytes 524320 | tf_op jit(solution)/shard_map/ppermute | solution.py:29
  64.3 8.3 %collective-permute-done.2 = bf16[2,256,512]{2,1,0:T(8,128)(2,1)} collective-permute-done((bf16[2,256,512]{2,1,0:T(8,128)(2,1)S(1)}, bf16[2,256,512]{2,1,0:T(8,128)(2,1)}, u32[]{:S(2)}, u32[]{:S(2)}) %collective-permute-start.2) | collective-permute-done | bytes 524320 | tf_op jit(solution)/shard_map/ppermute | solution.py:29
  75.5 8.3 %collective-permute-done.3 = bf16[2,256,512]{2,1,0:T(8,128)(2,1)} collective-permute-done((bf16[2,256,512]{2,1,0:T(8,128)(2,1)S(1)}, bf16[2,256,512]{2,1,0:T(8,128)(2,1)}, u32[]{:S(2)}, u32[]{:S(2)}) %collective-permute-start.3) | collective-permute-done | bytes 524320 | tf_op jit(solution)/shard_map/ppermute | solution.py:29
  85.1 54.2 %collective-permute-done.4 = bf16[2,256,512]{2,1,0:T(8,128)(2,1)} collective-permute-done((bf16[2,256,512]{2,1,0:T(8,128)(2,1)S(1)}, bf16[2,256,512]{2,1,0:T(8,128)(2,1)}, u32[]{:S(2)}, u32[]{:S(2)}) %collective-permute-start.4) | collective-permute-done | bytes 524320 | tf_op jit(solution)/shard_map/ppermute | solution.py:29
  149.6 6.2 %copy.99 = bf16[4,2,2048,128]{3,2,1,0:T(8,128)(2,1)} copy(bf16[4,2,2048,128]{2,3,0,1:T(8,128)(2,1)} %bitcast.20) | data formatting | bytes 8388608
  156.5 42.8 %while.25 = (s32[]{:T(128)}, bf16[4,256,128]{1,2,0:T(8,128)(2,1)}, bf16[4,2,2048,128]{2,3,0,1:T(8,128)(2,1)}, bf16[4,256,128]{2,1,0:T(8,128)(2,1)S(1)}, bf16[4,2...) while((s32[]{:T(128)}, bf16[4,256,128]{1,2,0:T(8,128)(2,1)}, ...), condition=%wide.region_8.9_spmd.clone, body=%wide.region_4.8_spmd.clone.sunk | while | flops 706772224 | bytes 27380468 | solution.py:92
  156.5 1.9 fusion.99
  167.2 1.9 fusion.99
  177.8 1.9 fusion.99
  199.3 3.5 fusion.59
  202.7 2.3 collective-permute-start.12
  205.0 3.0 collective-permute-start.11
  208.0 12.5 %collective-permute-done.14 = bf16[2,256,512]{1,2,0:T(8,128)(2,1)S(1)} collective-permute-done((bf16[2,256,512]{1,2,0:T(8,128)(2,1)S(1)}, bf16[2,256,512]{1,2,0:T(8,128)(2,1)S(1)}, u32[]{:S(2)}, u32[]{:S(2)}) %collective-permute-start.14) | collective-permute-done | bytes 524320 | tf_op jit(solution)/shard_map/ppermute | solution.py:29
  220.5 10.7 %collective-permute-start.8 = (bf16[2,256,512]{1,2,0:T(8,128)(2,1)S(1)}, bf16[2,256,512]{1,2,0:T(8,128)(2,1)}, u32[]{:S(2)}, u32[]{:S(2)}) collective-permute-start(bf16[2,256,512]{1,2,0:T(8,128)(2,1)S(1)} %get-tuple-element.306), channel_id=1, source_target_pairs={{0,28},{4,0},{8,4},{12,8},{16,12},{20,16},{24,20},{28,24},{1,29},{... | collective-permute-start | bytes 1572872 | tf_op jit(solution)/shard_map/ppermute | solution.py:29
  231.2 16.3 %while.24 = (s32[]{:T(128)}, bf16[4,256,128]{1,2,0:T(8,128)(2,1)S(1)}, bf16[4,256,128]{2,1,0:T(8,128)(2,1)S(1)}, bf16[4,2,2048,128]{3,2,1,0:T(8,128)(2,1)}, s32[...) while((s32[]{:T(128)}, ...), condition=%wide.region_3.4_spmd.clone, body=%wide.region_0.3_spmd.clone.sunk | while | flops 297827840 | bytes 7761061 | solution.py:89
  231.2 1.9 fusion.91
  235.3 1.9 fusion.91
  239.4 1.9 fusion.91
  243.4 1.9 fusion.91
  247.5 16.2 %collective-permute-done.12 = bf16[2,256,512]{1,2,0:T(8,128)(2,1)} collective-permute-done((bf16[2,256,512]{1,2,0:T(8,128)(2,1)}, bf16[2,256,512]{1,2,0:T(8,128)(2,1)}, u32[]{:S(2)}, u32[]{:S(2)}) %collective-permute-start.12) | collective-permute-done | bytes 524320 | tf_op jit(solution)/shard_map/ppermute | solution.py:29
  263.7 6.1 %collective-permute-done.8 = bf16[2,256,512]{1,2,0:T(8,128)(2,1)} collective-permute-done((bf16[2,256,512]{1,2,0:T(8,128)(2,1)S(1)}, bf16[2,256,512]{1,2,0:T(8,128)(2,1)}, u32[]{:S(2)}, u32[]{:S(2)}) %collective-permute-start.8) | collective-permute-done | bytes 524320 | tf_op jit(solution)/shard_map/ppermute | solution.py:29
  269.9 2.7 add_convert_fusion
  273.7 4.6 %all_to_all.31 = bf16[4,256,512]{2,0,1:T(4,128)(2,1)S(1)} all-to-all(bf16[4,256,512]{2,0,1:T(4,128)(2,1)S(1)} %copy.107), channel_id=1, replica_groups=mesh['rep'=1,'seq'=8,'head'=2,'sub'=2] {'sub'}, dimensions={1} | all-to-all | bytes 2097152 | tf_op jit(solution)/shard_map/all_to_all | solution.py:154
  280.1 5.1 %psum.22 = f32[128,16]{0,1:T(8,128)S(1)} all-reduce(f32[128,16]{0,1:T(8,128)S(1)} %fusion.63), channel_id=1, replica_groups=mesh['rep'=1,'seq'=8,'head'=2,'sub'=2] {'head'}, use_global_device_ids=true, to_apply=%region_10.11 | all-reduce | flops 2048 | bytes 16384 | tf_op jit(solution)/shard_map/psum | solution.py:165
  289.3 111.7 %all-reduce.3.cloned.1.call-done = (f32[1024,16]{0,1:T(8,128)}, f32[16,2048]{1,0:T(8,128)}) async-done(((f32[1024,16]{0,1:T(8,128)}, f32[16,2048]{1,0:T(8,128)}), (f32[1024,16]{0,1:T(8,128)}, f32[16,2048]{1,0:T(8,128)})) %all-reduce.3.cloned.1.call-update) | async-done | bytes 196624 | tf_op jit(solution)/shard_map/psum | solution.py:169
  (182 shorter events, 79.7 us)
Async XLA Ops:
  7.2 16.5 %copy-start = (bf16[16,4096]{1,0:T(8,128)(2,1)S(1)}, bf16[16,4096]{1,0:T(8,128)(2,1)}, u32[]{:S(2)}) copy-start(bf16[16,4096]{1,0:T(8,128)(2,1)} %param.17) | copy-start | bytes 393220
  7.2 25.0 %all-gather.2.cloned.1.call-start = ((), (), s32[]{:S(2)}) async-start(), calls=%async_computation.2 | async-start | bytes 12582912 | tf_op jit(solution)/shard_map/all_gather | solution.py:117
  7.9 393.1 %all-reduce.3.cloned.1.call-start = ((), (), s32[]{:S(2)}) async-start(), calls=%async_computation.3 | async-start | bytes 393216 | tf_op jit(solution)/shard_map/psum | solution.py:169
  8.5 14.9 %collective-permute-start = (bf16[1,128,2048]{1,2,0:T(8,128)(2,1)S(1)}, bf16[1,128,2048]{1,2,0:T(8,128)(2,1)S(1)}, u32[]{:S(2)}, u32[]{:S(2)}) collective-permute-start(bf16[1,128,2048]{1,2,0:T(8,128)(2,1)S(1)} %bitcast.152), channel_id=1, source_target_pairs={{0,2},{2,0},{1,3},{3,1},{4,6},{6,4},{5,7},{7,5},{8,10},{10,8},{9,1... | collective-permute-start | bytes 1572872 | tf_op jit(solution)/shard_map/ppermute | solution.py:20
  25.0 13.5 %copy-start.7 = (bf16[128,1024]{1,0:T(8,128)(2,1)S(1)}, bf16[128,1024]{1,0:T(8,128)(2,1)}, u32[]{:S(2)}) copy-start(bf16[128,1024]{1,0:T(8,128)(2,1)} %param.13) | copy-start | bytes 786436
  25.0 13.5 %copy-start.8 = (bf16[128,1024]{1,0:T(8,128)(2,1)S(1)}, bf16[128,1024]{1,0:T(8,128)(2,1)}, u32[]{:S(2)}) copy-start(bf16[128,1024]{1,0:T(8,128)(2,1)} %param.12) | copy-start | bytes 786436
  25.0 13.5 %copy-start.9 = (bf16[128,1024]{1,0:T(8,128)(2,1)S(1)}, bf16[128,1024]{1,0:T(8,128)(2,1)}, u32[]{:S(2)}) copy-start(bf16[128,1024]{1,0:T(8,128)(2,1)} %param.11) | copy-start | bytes 786436
  44.4 16.9 %collective-permute-start.1 = (bf16[2,256,512]{2,1,0:T(8,128)(2,1)S(1)}, bf16[2,256,512]{2,1,0:T(8,128)(2,1)S(1)}, u32[]{:S(2)}, u32[]{:S(2)}) collective-permute-start(bf16[2,256,512]{2,1,0:T(8,128)(2,1)S(1)} %bitcast.167), channel_id=1, source_target_pairs={{0,28},{4,0},{8,4},{12,8},{16,12},{20,16},{24,20},{28,24},{1,29},{... | collective-permute-start | bytes 1572872 | tf_op jit(solution)/shard_map/ppermute | solution.py:29
  48.9 23.6 %collective-permute-start.2 = (bf16[2,256,512]{2,1,0:T(8,128)(2,1)S(1)}, bf16[2,256,512]{2,1,0:T(8,128)(2,1)}, u32[]{:S(2)}, u32[]{:S(2)}) collective-permute-start(bf16[2,256,512]{2,1,0:T(8,128)(2,1)S(1)} %bitcast.168), channel_id=1, source_target_pairs={{0,24},{4,28},{8,0},{12,4},{16,8},{20,12},{24,16},{28,20},{1,25},{... | collective-permute-start | bytes 1572872 | tf_op jit(solution)/shard_map/ppermute | solution.py:29
  50.7 33.1 %collective-permute-start.3 = (bf16[2,256,512]{2,1,0:T(8,128)(2,1)S(1)}, bf16[2,256,512]{2,1,0:T(8,128)(2,1)}, u32[]{:S(2)}, u32[]{:S(2)}) collective-permute-start(bf16[2,256,512]{2,1,0:T(8,128)(2,1)S(1)} %bitcast.169), channel_id=1, source_target_pairs={{0,20},{4,24},{8,28},{12,0},{16,4},{20,8},{24,12},{28,16},{1,21},{... | collective-permute-start | bytes 1572872 | tf_op jit(solution)/shard_map/ppermute | solution.py:29
  50.7 88.5 %collective-permute-start.4 = (bf16[2,256,512]{2,1,0:T(8,128)(2,1)S(1)}, bf16[2,256,512]{2,1,0:T(8,128)(2,1)}, u32[]{:S(2)}, u32[]{:S(2)}) collective-permute-start(bf16[2,256,512]{2,1,0:T(8,128)(2,1)S(1)} %bitcast.170), channel_id=1, source_target_pairs={{0,16},{4,20},{8,24},{12,28},{16,0},{20,4},{24,8},{28,12},{1,17},{... | collective-permute-start | bytes 1572872 | tf_op jit(solution)/shard_map/ppermute | solution.py:29
  53.6 86.9 %collective-permute-start.5 = (bf16[2,256,512]{2,1,0:T(8,128)(2,1)S(1)}, bf16[2,256,512]{2,1,0:T(8,128)(2,1)}, u32[]{:S(2)}, u32[]{:S(2)}) collective-permute-start(bf16[2,256,512]{2,1,0:T(8,128)(2,1)S(1)} %bitcast.171), channel_id=1, source_target_pairs={{0,12},{4,16},{8,20},{12,24},{16,28},{20,0},{24,4},{28,8},{1,13},{... | collective-permute-start | bytes 1572872 | tf_op jit(solution)/shard_map/ppermute | solution.py:29
  61.3 80.5 %collective-permute-start.6 = (bf16[2,256,512]{2,1,0:T(8,128)(2,1)S(1)}, bf16[2,256,512]{2,1,0:T(8,128)(2,1)}, u32[]{:S(2)}, u32[]{:S(2)}) collective-permute-start(bf16[2,256,512]{2,1,0:T(8,128)(2,1)S(1)} %bitcast.172), channel_id=1, source_target_pairs={{0,8},{4,12},{8,16},{12,20},{16,24},{20,28},{24,0},{28,4},{1,9},{5... | collective-permute-start | bytes 1572872 | tf_op jit(solution)/shard_map/ppermute | solution.py:29
  72.5 74.0 %collective-permute-start.7 = (bf16[2,256,512]{2,1,0:T(8,128)(2,1)S(1)}, bf16[2,256,512]{2,1,0:T(8,128)(2,1)}, u32[]{:S(2)}, u32[]{:S(2)}) collective-permute-start(bf16[2,256,512]{2,1,0:T(8,128)(2,1)S(1)} %bitcast.173), channel_id=1, source_target_pairs={{0,4},{4,8},{8,12},{12,16},{16,20},{20,24},{24,28},{28,0},{1,5},{5... | collective-permute-start | bytes 1572872 | tf_op jit(solution)/shard_map/ppermute | solution.py:29
  156.5 1.9 copy-start.14
  167.2 1.9 copy-start.14
  177.8 1.9 copy-start.14
  188.5 1.9 copy-start.14
  197.6 1.7 copy-start.15
  202.7 17.8 %collective-permute-start.14 = (bf16[2,256,512]{1,2,0:T(8,128)(2,1)S(1)}, bf16[2,256,512]{1,2,0:T(8,128)(2,1)S(1)}, u32[]{:S(2)}, u32[]{:S(2)}) collective-permute-start(bf16[2,256,512]{1,2,0:T(8,128)(2,1)S(1)} %get-tuple-element.307), channel_id=1, source_target_pairs={{0,4},{4,8},{8,12},{12,16},{16,20},{20,24},{24,28},{28,0},{1,5},{5... | collective-permute-start | bytes 1572872 | tf_op jit(solution)/shard_map/ppermute | solution.py:29
  202.7 17.8 %collective-permute-start.13 = (bf16[2,256,512]{1,2,0:T(8,128)(2,1)S(1)}, bf16[2,256,512]{1,2,0:T(8,128)(2,1)S(1)}, u32[]{:S(2)}, u32[]{:S(2)}) collective-permute-start(bf16[2,256,512]{1,2,0:T(8,128)(2,1)S(1)} %get-tuple-element.308), channel_id=1, source_target_pairs={{0,8},{4,12},{8,16},{12,20},{16,24},{20,28},{24,0},{28,4},{1,9},{5... | collective-permute-start | bytes 1572872 | tf_op jit(solution)/shard_map/ppermute | solution.py:29
  202.7 61.0 %collective-permute-start.12 = (bf16[2,256,512]{1,2,0:T(8,128)(2,1)}, bf16[2,256,512]{1,2,0:T(8,128)(2,1)}, u32[]{:S(2)}, u32[]{:S(2)}) collective-permute-start(bf16[2,256,512]{1,2,0:T(8,128)(2,1)} %get-tuple-element.309), channel_id=1, source_target_pairs={{0,12},{4,16},{8,20},{12,24},{16,28},{20,0},{24,4},{28,8},{1,13},{... | collective-permute-start | bytes 1572872 | tf_op jit(solution)/shard_map/ppermute | solution.py:29
  205.0 58.7 %collective-permute-start.11 = (bf16[2,256,512]{1,2,0:T(8,128)(2,1)}, bf16[2,256,512]{1,2,0:T(8,128)(2,1)}, u32[]{:S(2)}, u32[]{:S(2)}) collective-permute-start(bf16[2,256,512]{1,2,0:T(8,128)(2,1)} %get-tuple-element.310), channel_id=1, source_target_pairs={{0,16},{4,20},{8,24},{12,28},{16,0},{20,4},{24,8},{28,12},{1,17},{... | collective-permute-start | bytes 1572872 | tf_op jit(solution)/shard_map/ppermute | solution.py:29
  208.0 55.7 %collective-permute-start.10 = (bf16[2,256,512]{1,2,0:T(8,128)(2,1)}, bf16[2,256,512]{1,2,0:T(8,128)(2,1)}, u32[]{:S(2)}, u32[]{:S(2)}) collective-permute-start(bf16[2,256,512]{1,2,0:T(8,128)(2,1)} %get-tuple-element.311), channel_id=1, source_target_pairs={{0,20},{4,24},{8,28},{12,0},{16,4},{20,8},{24,12},{28,16},{1,21},{... | collective-permute-start | bytes 1572872 | tf_op jit(solution)/shard_map/ppermute | solution.py:29
  220.5 10.7 %copy-start.5 = (bf16[2,256,512]{1,2,0:T(8,128)(2,1)}, bf16[2,256,512]{1,2,0:T(8,128)(2,1)S(1)}, u32[]{:S(2)}) copy-start(bf16[2,256,512]{1,2,0:T(8,128)(2,1)S(1)} %collective-permute-done.14) | copy-start | bytes 1572868
  220.5 43.3 %collective-permute-start.9 = (bf16[2,256,512]{1,2,0:T(8,128)(2,1)}, bf16[2,256,512]{1,2,0:T(8,128)(2,1)}, u32[]{:S(2)}, u32[]{:S(2)}) collective-permute-start(bf16[2,256,512]{1,2,0:T(8,128)(2,1)} %get-tuple-element.312), channel_id=1, source_target_pairs={{0,24},{4,28},{8,0},{12,4},{16,8},{20,12},{24,16},{28,20},{1,25},{... | collective-permute-start | bytes 1572872 | tf_op jit(solution)/shard_map/ppermute | solution.py:29
  220.5 10.7 %copy-start.6 = (bf16[2,256,512]{1,2,0:T(8,128)(2,1)}, bf16[2,256,512]{1,2,0:T(8,128)(2,1)S(1)}, u32[]{:S(2)}) copy-start(bf16[2,256,512]{1,2,0:T(8,128)(2,1)S(1)} %collective-permute-done.13) | copy-start | bytes 1572868
  220.5 49.4 %collective-permute-start.8 = (bf16[2,256,512]{1,2,0:T(8,128)(2,1)S(1)}, bf16[2,256,512]{1,2,0:T(8,128)(2,1)}, u32[]{:S(2)}, u32[]{:S(2)}) collective-permute-start(bf16[2,256,512]{1,2,0:T(8,128)(2,1)S(1)} %get-tuple-element.306), channel_id=1, source_target_pairs={{0,28},{4,0},{8,4},{12,8},{16,12},{20,16},{24,20},{28,24},{1,29},{... | collective-permute-start | bytes 1572872 | tf_op jit(solution)/shard_map/ppermute | solution.py:29
  247.5 25.0 %copy-start.4 = (bf16[4,256,128]{1,2,0:T(8,128)(2,1)S(1)}, bf16[4,256,128]{1,2,0:T(8,128)(2,1)}, u32[]{:S(2)}) copy-start(bf16[4,256,128]{1,2,0:T(8,128)(2,1)} %get-tuple-element.71) | copy-start | bytes 786436
  278.3 1.6 copy-start.11
  278.5 6.7 %copy-start.3 = (bf16[128,2048]{1,0:T(8,128)(2,1)S(1)}, bf16[128,2048]{1,0:T(8,128)(2,1)}, u32[]{:S(2)}) copy-start(bf16[128,2048]{1,0:T(8,128)(2,1)} %param.14) | copy-start | bytes 1572868
  280.1 124.0 %copy-start.1 = (bf16[16,4096]{1,0:T(8,128)(2,1)S(1)}, bf16[16,4096]{1,0:T(8,128)(2,1)}, u32[]{:S(2)}) copy-start(bf16[16,4096]{1,0:T(8,128)(2,1)} %param.17) | copy-start | bytes 393220
  (7 other events, 8.2 us)
Sparse Core Ops, SparseCore 0:
  9.6 22.5 all-gather.1
  286.3 114.6 all-reduce.2
